TPU v7x, 128 devices: a whole 4x4x4 slice. The times are simulated.
128 devices in a mesh: frame: 64 (over z, y, x), pix: 2 (over core).
Axes of the slice: x: 4, y: 4, z: 4, core: 2. Of those that a mesh axis runs over, the one named last changes fastest.
Arguments:
- frames: bfloat16 [1024, 131072], P('frame', 'pix'), as said below
- cycle_map: int32 [131072], P('pix'), may hold values from -1 to 63, as said below
Outputs:
- correlation: bfloat16 [64, 1024, 1024], P('frame', 'pix')
Inputs may be any that keep to these rules, and one draw needn't show every extreme that they name: `frames`: every entry is positive. `cycle_map`: pixels come in aligned blocks of 128; every pixel of a block is either -1 or one common cycle, and the first pixel of a block that holds a cycle belongs to it. Within each sector (aligned blocks of 65536 pixels, one a pix group) every cycle holds at least one and at most 8 blocks, and every cycle holds exactly 1024 pixels in some sector.
All inputs are finite; a program needn't handle non-finite values.
Results may differ from a plain program's by a relative error of at most 0.012.
Values may be sent and summed in bfloat16 or wider, within the bound.
A program may use at most 64 MiB of HBM per device.

v0:
```python
import jax
import jax.numpy as jnp
from jax import lax
from jax.sharding import PartitionSpec as P

BLOCK = 128
HALF_WIN = 2


def with_halo(value, sides, width):
    for axis, dim in sides:
        peers, length = (lax.axis_size(axis), value.shape[dim])
        up = [(i, (i + 1) % peers) for i in range(peers - 1)]
        down = [(j, i) for i, j in up]
        last = lax.slice_in_dim(value, length - width, length, axis=dim)
        initial = lax.slice_in_dim(value, 0, width, axis=dim)
        before = lax.ppermute(last, axis, up)
        after = lax.ppermute(initial, axis, down)
        value = jnp.concatenate([before, value, after], axis=dim)
    return value


def window_sum(padded, length):
    summed = padded[0:length]
    for offset in range(1, 2 * HALF_WIN + 1):
        summed = summed + padded[offset : offset + length]
    return summed


def smooth_count(first_frame, length, total):
    frame_pos = first_frame + jnp.arange(length, dtype=jnp.int32)
    upper = jnp.minimum(frame_pos + HALF_WIN, total - 1)
    lower = jnp.maximum(frame_pos - HALF_WIN, 0)
    return (upper - lower + 1).astype(jnp.float32)


def body(frames, cycle_map):
    fr_dev, p_sec = frames.shape
    cycles = lax.axis_size("frame")
    cap = p_sec // cycles
    total = fr_dev * cycles
    block_count = p_sec // BLOCK
    cap_blocks = cap // BLOCK
    cycle_blocks = cycle_map.reshape(block_count, BLOCK)
    pixel_valid = cycle_blocks >= 0
    block_cycle = jnp.max(cycle_blocks, axis=1)
    cycle_ids = jnp.arange(cycles, dtype=jnp.int32)
    member = (block_cycle[:, None] == cycle_ids[None, :]).astype(jnp.bfloat16)
    block_pos = jnp.arange(block_count, dtype=jnp.int32)
    earlier = (block_pos[None, :] < block_pos[:, None]).astype(jnp.bfloat16)
    before = jnp.dot(earlier, member, preferred_element_type=jnp.float32)
    block_rank = jnp.sum(before * member.astype(jnp.float32), axis=1).astype(jnp.int32)
    block_slot = block_cycle * cap_blocks + block_rank
    slot_ids = jnp.arange(cycles * cap_blocks, dtype=jnp.int32)
    selector = ((block_slot[None, :] == slot_ids[:, None]) & (block_cycle[None, :] >= 0)).astype(
        jnp.bfloat16
    )
    valid_count = jnp.sum(pixel_valid.astype(jnp.float32), axis=1)
    counts = jnp.sum(member.astype(jnp.float32) * valid_count[:, None], axis=0)
    own_index = lax.axis_index("frame")
    own_count = lax.dynamic_index_in_dim(counts, own_index, 0, keepdims=False)
    padded = with_halo(frames, (("frame", 0),), HALF_WIN).astype(jnp.float32)
    summed = window_sum(padded, fr_dev)
    divisor = smooth_count(own_index * fr_dev, fr_dev, total)
    local_mean = summed / divisor[:, None]
    source = (frames.astype(jnp.float32) / local_mean).astype(jnp.bfloat16)
    masked = jnp.where(cycle_map[None, :] >= 0, source, jnp.zeros((), jnp.bfloat16))
    grouped = masked.reshape(fr_dev, block_count, BLOCK)
    picked = jnp.einsum("sb,tbc->tsc", selector, grouped, preferred_element_type=jnp.float32)
    picked = picked.astype(jnp.bfloat16).reshape(fr_dev, cycles * cap)
    received = lax.all_to_all(picked, "frame", split_axis=1, concat_axis=0, tiled=True)
    row_count = total // lax.axis_size("pix")
    first_row = lax.axis_index("pix") * row_count
    gram_part = lax.psum_scatter(
        lax.dot_general(
            received, received, (((1,), (1,)), ((), ())), preferred_element_type=jnp.float32
        ),
        "pix",
        scatter_dimension=0,
        tiled=True,
    )
    frame_sums, number = lax.psum((jnp.sum(received, axis=1, dtype=jnp.float32), own_count), "pix")
    row_sums = lax.dynamic_slice_in_dim(frame_sums, first_row, row_count, 0)
    result = number * gram_part / (row_sums[:, None] * frame_sums[None, :]) - 1.0
    return result.astype(jnp.bfloat16)[None]


def solution(mesh):
    return jax.shard_map(
        body,
        mesh=mesh,
        in_specs=(P("frame", "pix"), P("pix")),
        out_specs=P("frame", "pix", None),
        check_vma=False,
    )
```

profile of v0, /device:TPU:1, one launch (start us, length us, event | category | flops | bytes accessed | tf_op | source)
XLA Modules:
  0.0 107.2 jit_solution(4033306784305556422)
XLA Ops:
  6.5 0.0 copy-start
  6.5 0.0 reduce-scatter.2.cloned.1.call-start
  6.5 2.1 %fusion.12 = (bf16[2,65536]{1,0:T(2,128)(2,1)S(1)}, bf16[2,65536]{1,0:T(2,128)(2,1)S(1)}) fusion(bf16[16,65536]{1,0:T(8,128)(2,1)} %param.2), kind=kLoop, calls=%fused_computation.32 | loop fusion | bytes 1048576 | tf_op jit(solution)/shard_map/slice | solution.py:15
  8.6 4.0 %collective-permute-start = (bf16[2,65536]{1,0:T(2,128)(2,1)S(1)}, bf16[2,65536]{1,0:T(2,128)(2,1)S(1)}, u32[]{:S(2)}, u32[]{:S(2)}) collective-permute-start(bf16[2,65536]{1,0:T(2,128)(2,1)S(1)} %get-tuple-element.7), channel_id=1, source_target_pairs={{0,2},{2,4},{4,6},{6,8},{8,10},{10,12},{12,14},{14,16},{16,18},{18... | collective-permute-start | bytes 786440 | tf_op jit(solution)/shard_map/ppermute | solution.py:17
  12.6 1.3 %collective-permute-start.1 = (bf16[2,65536]{1,0:T(2,128)(2,1)S(1)}, bf16[2,65536]{1,0:T(2,128)(2,1)S(1)}, u32[]{:S(2)}, u32[]{:S(2)}) collective-permute-start(bf16[2,65536]{1,0:T(2,128)(2,1)S(1)} %get-tuple-element.8), channel_id=1, source_target_pairs={{2,0},{4,2},{6,4},{8,6},{10,8},{12,10},{14,12},{16,14},{18,16},{20... | collective-permute-start | bytes 786440 | tf_op jit(solution)/shard_map/ppermute | solution.py:18
  13.9 1.0 broadcast_compare_fusion
  14.9 1.1 %bitcast_reduce_fusion = s32[512]{0:T(512)S(1)} fusion(s32[65536]{0:T(1024)} %param.3), kind=kLoop, calls=%fused_computation.21 | loop fusion | flops 65024 | bytes 264192 | tf_op jit(solution)/shard_map/reduce_max | solution.py:46
  16.0 0.3 fusion.2
  16.3 1.2 %collective-permute-done = bf16[2,65536]{1,0:T(2,128)(2,1)S(1)} collective-permute-done((bf16[2,65536]{1,0:T(2,128)(2,1)S(1)}, bf16[2,65536]{1,0:T(2,128)(2,1)S(1)}, u32[]{:S(2)}, u32[]{:S(2)}) %collective-permute-start) | collective-permute-done | bytes 262176 | tf_op jit(solution)/shard_map/ppermute | solution.py:17
  17.5 3.8 %collective-permute-done.1 = bf16[2,65536]{1,0:T(2,128)(2,1)S(1)} collective-permute-done((bf16[2,65536]{1,0:T(2,128)(2,1)S(1)}, bf16[2,65536]{1,0:T(2,128)(2,1)S(1)}, u32[]{:S(2)}, u32[]{:S(2)}) %collective-permute-start.1) | collective-permute-done | bytes 262176 | tf_op jit(solution)/shard_map/ppermute | solution.py:18
  21.4 0.0 copy-done
  21.4 1.1 %maximum_convert_fusion = f32[20,65536]{1,0:T(8,128)S(1)} fusion(bf16[2,65536]{1,0:T(2,128)(2,1)S(1)} %collective-permute-done.1, bf16[16,65536]{1,0:T(8,128)(2,1)S(1)} %copy-done, bf16[2,65536]{1,0:T(2,128)(2,1)S(1)} %collective-permute-done), kind=kLoop, calls=%fused_computation.7 | loop fusion | flops 7864320 | bytes 7864320 | tf_op jit(solution)/shard_map/convert_element_type | solution.py:62
  22.4 2.7 %select_bitcast_fusion = bf16[2,8,512,128]{3,1,2,0:T(8,128)(2,1)S(1)} fusion(pred[65536]{0:T(1024)(128)(4,1)S(1)} %broadcast_compare_fusion, f32[20,65536]{1,0:T(8,128)S(1)} %maximum_convert_fusion, f32[16]{0:T(128)S(1)} %add_convert_fusion.1, bf16[16,65536]{1,0:T(8,128)(2,1)S(1)} %copy-done), kind=kLoop, calls=%fused_computation.10 | loop fusion | flops 9437184 | bytes 25231424
  25.1 0.4 copy.19
  25.5 2.7 %convert_bitcast_fusion = bf16[16,512,128]{1,2,0:T(8,128)(2,1)} fusion(bf16[16,512,128]{2,1,0:T(8,128)(2,1)S(1)} %bitcast.24, s32[512]{0:T(512)S(1)} %convert_add_fusion, pred[512]{0:T(512)(128)(4,1)S(1)} %broadcast_compare_fusion.1), kind=kOutput, calls=%fused_computation.9 | convolution fusion | flops 1075314688 | bytes 4196864 | tf_op jit(solution)/shard_map/sb,tbc->tsc/dot_general | solution.py:69
  28.2 3.0 %copy.13 = bf16[16,512,128]{2,1,0:T(8,128)(2,1)S(1)} copy(bf16[16,512,128]{1,2,0:T(8,128)(2,1)} %convert_bitcast_fusion) | data formatting | bytes 4194304 | tf_op jit(solution)/shard_map/convert_element_type | solution.py:70
  31.3 2.3 %all_to_all.14 = bf16[16,64,1024]{2,1,0:T(8,128)(2,1)} reshape(bf16[16,512,128]{2,1,0:T(8,128)(2,1)S(1)} %copy.13) | data formatting | bytes 4194304 | tf_op jit(solution)/shard_map/all_to_all | solution.py:71
  33.6 2.7 %copy.14 = bf16[16,64,1024]{2,0,1:T(8,128)(2,1)S(1)} copy(bf16[16,64,1024]{2,1,0:T(8,128)(2,1)} %all_to_all.14) | data formatting | bytes 4194304 | tf_op jit(solution)/shard_map/all_to_all | solution.py:71
  36.3 41.8 %all_to_all.19 = bf16[16,64,1024]{2,0,1:T(8,128)(2,1)S(1)} all-to-all(bf16[16,64,1024]{2,0,1:T(8,128)(2,1)S(1)} %copy.14), channel_id=1, replica_groups=mesh['frame'=64,'pix'=2] {'frame'}, dimensions={1} | all-to-all | bytes 4194304 | tf_op jit(solution)/shard_map/all_to_all | solution.py:71
  78.2 4.3 %fusion.13 = f32[1024,1024]{1,0:T(8,128)} fusion(bf16[1024,1024]{1,0:T(8,128)(2,1)S(1)} %bitcast.23), kind=kOutput, calls=%fused_computation.33 | convolution fusion | flops 2147483648 | bytes 6291456 | tf_op jit(solution)/shard_map/dot_general | solution.py:75
  82.5 0.0 copy-start.1
  82.5 0.0 reduce-scatter.2.cloned.1.call-update
  82.5 0.9 copy-done.1
  83.4 0.1 convert_reduce_fusion.1
  83.5 0.1 fusion.9
  83.7 0.6 dynamic_slice.7
  84.2 0.3 convert_reduce_fusion
  84.6 0.1 reduce_sum.42
  84.7 6.1 %all-reduce = (f32[1024]{0:T(1024)S(1)}, f32[]{:T(128)}) all-reduce(f32[1024]{0:T(1024)S(1)} %reduce_sum.42, f32[]{:T(128)} %bitcast.1), channel_id=1, replica_groups=mesh['frame'=64,'pix'=2] {'pix'}, use_global_device_ids=true, to_apply=%region_7.8 | all-reduce | flops 1025 | bytes 8200 | tf_op jit(solution)/shard_map/psum | solution.py:82
  90.7 0.1 dynamic_slice.8
  90.8 6.0 %reduce-scatter.2.cloned.1.call-done = f32[512,1024]{1,0:T(8,128)} async-done(((f32[1024,1024]{1,0:T(8,128)}), f32[512,1024]{1,0:T(8,128)}) %reduce-scatter.2.cloned.1.call-update) | async-done | bytes 2097168 | tf_op jit(solution)/shard_map/reduce_scatter | solution.py:74
  96.8 3.6 %fusion.3 = bf16[1,512,1024]{2,1,0:T(8,128)(2,1)} fusion(f32[1024]{0:T(1024)S(1)} %get-tuple-element.5, f32[512]{0:T(512)S(1)} %dynamic_slice.8, f32[512,1024]{1,0:T(8,128)} %reduce-scatter.2.cloned.1.call-done, f32[]{:T(128)} %get-tuple-element.6), kind=kLoop, calls=%fused_computation.15 | loop fusion | flops 2621440 | bytes 3151876 | tf_op jit(solution)/shard_map/broadcast_in_dim | solution.py:85
  (3 shorter events, 0.0 us)
Async XLA Ops:
  6.5 14.8 %copy-start = (bf16[16,65536]{1,0:T(8,128)(2,1)S(1)}, bf16[16,65536]{1,0:T(8,128)(2,1)}, u32[]{:S(2)}) copy-start(bf16[16,65536]{1,0:T(8,128)(2,1)} %param.2) | copy-start | bytes 6291460
  6.5 90.3 %reduce-scatter.2.cloned.1.call-start = ((), (), s32[]{:S(2)}) async-start(), calls=%async_computation.2 | async-start | bytes 6291456 | tf_op jit(solution)/shard_map/reduce_scatter | solution.py:74
  8.6 8.9 %collective-permute-start = (bf16[2,65536]{1,0:T(2,128)(2,1)S(1)}, bf16[2,65536]{1,0:T(2,128)(2,1)S(1)}, u32[]{:S(2)}, u32[]{:S(2)}) collective-permute-start(bf16[2,65536]{1,0:T(2,128)(2,1)S(1)} %get-tuple-element.7), channel_id=1, source_target_pairs={{0,2},{2,4},{4,6},{6,8},{8,10},{10,12},{12,14},{14,16},{16,18},{18... | collective-permute-start | bytes 786440 | tf_op jit(solution)/shard_map/ppermute | solution.py:17
  12.6 8.8 %collective-permute-start.1 = (bf16[2,65536]{1,0:T(2,128)(2,1)S(1)}, bf16[2,65536]{1,0:T(2,128)(2,1)S(1)}, u32[]{:S(2)}, u32[]{:S(2)}) collective-permute-start(bf16[2,65536]{1,0:T(2,128)(2,1)S(1)} %get-tuple-element.8), channel_id=1, source_target_pairs={{2,0},{4,2},{6,4},{8,6},{10,8},{12,10},{14,12},{16,14},{18,16},{20... | collective-permute-start | bytes 786440 | tf_op jit(solution)/shard_map/ppermute | solution.py:18
  82.5 0.9 copy-start.1
Sparse Core Ops, SparseCore 0:
  82.6 14.1 reduce-scatter.1
where the time goes:
time: 108 us; the launch traced here: 107 us
  blocking collectives  47.9 us (44%)
  between operations  13.5 us (12%)
  local copies, waits for them, and re-layouts  12.2 us (11%)
  waiting for transfers between devices  11 us (10%)
  other arithmetic  10 us (9%)
  matrix products  7.29 us (7%)
  starting transfers between devices  5.25 us (5%)
    all_to_all x1, blocking collectives, body(): lax.all_to_all(picked, 'frame', split_axis=1, concat_axis=0, tiled=True)  41.8 us
    psum x1, blocking collectives, body(): lax.psum((jnp.sum(received, axis=1, dtype=jnp.float32), own_count), 'pix')  6.08 us
    reduce_scatter x1, waiting for transfers between devices, body(): lax.psum_scatter(lax.dot_general(received, received, (((1,), (1,)), ((),...  6 us
    all_to_all x2, local copies, waits for them, and re-layouts, body(): lax.all_to_all(picked, 'frame', split_axis=1, concat_axis=0, tiled=True)  5.07 us
    dot_general x1, matrix products, body(): lax.dot_general(received, received, (((1,), (1,)), ((), ())), preferred_e...  4.3 us
    ppermute x1, starting transfers between devices, with_halo(): before = lax.ppermute(last, axis, up)  3.96 us
    ppermute x1, waiting for transfers between devices, with_halo(): after = lax.ppermute(initial, axis, down)  3.81 us
    broadcast_in_dim x1, other arithmetic, body(): return result.astype(jnp.bfloat16)[None]  3.57 us
  transfers between devices with their start and end apart: 3, of which 3 were waited for; matrix products, arithmetic and copies ran while one was open for 3% of the time, Pallas kernels for 0%

commit v1 on v0

v1 whole, which is shorter than its diff:
```python
import functools

import jax
import jax.numpy as jnp
from jax import lax
from jax.experimental import pallas as pl
from jax.experimental.pallas import tpu as pltpu
from jax.sharding import PartitionSpec as P

BLOCK = 128
HALF_WIN = 2
PAD = 16
CHUNKS = 4
STRIDE = 27
MESH = pl.DeviceIdType.MESH


def kernel(
    cycles,
    frames_hbm,
    map_hbm,
    out_ref,
    fr,
    cmap,
    table_v,
    table,
    send,
    recv,
    own,
    oth,
    acc,
    rowacc,
    inv_len,
    band,
    mask,
    cnt_own,
    cnt_oth,
    load_sem,
    send_sem,
    recv_sem,
    swap_send,
    swap_recv,
    cnt_sem,
):
    f = lax.axis_index("frame")
    p = lax.axis_index("pix")
    fr_dev = frames_hbm.shape[0]
    p_sec = frames_hbm.shape[1]
    blocks = p_sec // BLOCK
    total = fr_dev * cycles
    rows = total // 2
    slots = p_sec // cycles // BLOCK
    per = slots // CHUNKS
    width = per * BLOCK
    tile = min(256, total)

    map_copy = pltpu.make_async_copy(map_hbm, cmap.at[pl.ds(0, blocks)], load_sem.at[0])
    map_copy.start()
    fr_copy = pltpu.make_async_copy(frames_hbm, fr.at[:, pl.ds(0, p_sec)], load_sem.at[1])
    fr_copy.start()

    barrier = pltpu.get_barrier_semaphore()

    def greet(i, carry):
        peer = lax.rem(f + STRIDE * i, cycles)
        pl.semaphore_signal(barrier, inc=1, device_id=(peer, p), device_id_type=MESH)
        return carry

    lax.fori_loop(1, cycles, greet, 0)
    pl.semaphore_signal(barrier, inc=1, device_id=(f, 1 - p), device_id_type=MESH)

    fr[:, pl.ds(p_sec, BLOCK)] = jnp.zeros((fr_dev, BLOCK), jnp.bfloat16)
    cmap[pl.ds(blocks, 8), :] = jnp.full((8, BLOCK), -1, jnp.int32)
    map_copy.wait()
    lane = lax.broadcasted_iota(jnp.int32, (8, BLOCK), 1)
    lead = lax.broadcasted_iota(jnp.int32, (8, BLOCK), 0)
    running = jnp.zeros((8, BLOCK), jnp.int32)
    member = []
    before = []
    for v in range(blocks // 8):
        member.append(jnp.broadcast_to(cmap[pl.ds(8 * v, 8), 0:1], (8, BLOCK)) == lane)
        before.append(running)
        running = running + jnp.where(member[v], 1, 0)
    ahead = [jnp.zeros((1, BLOCK), jnp.int32)]
    for i in range(7):
        ahead.append(ahead[i] + running[i : i + 1, :])
    ahead = jnp.concatenate(ahead, axis=0)
    picks = [jnp.zeros((8, BLOCK), jnp.int32)] * slots
    for v in range(blocks // 8):
        rank = jnp.where(member[v], before[v] + ahead, -1)
        for r in range(slots):
            picks[r] = picks[r] + jnp.where(rank == r, lead + (8 * v + 1), 0)
    found = jnp.concatenate([jnp.sum(x, axis=0, keepdims=True) for x in picks], axis=0)
    table_v[...] = jnp.where(found > 0, found - 1, blocks)
    table_copy = pltpu.make_async_copy(table_v, table, load_sem.at[2])
    table_copy.start()
    table_copy.wait()
    fr_copy.wait()

    def pick(k):
        def one(q, carry):
            for j in range(per):
                b = table[k * per + j, q]
                send[k, pl.ds(pl.multiple_of(q * fr_dev, fr_dev), fr_dev), pl.ds(j * BLOCK, BLOCK)] = fr[
                    :, pl.ds(b * BLOCK, BLOCK)
                ]
            return carry

        lax.fori_loop(0, cycles, one, 0, unroll=8 if cycles % 8 == 0 else 1)

    def ship(k):
        def one(i, carry):
            peer = lax.rem(f + STRIDE * i, cycles)
            pltpu.make_async_remote_copy(
                src_ref=send.at[k, pl.ds(pl.multiple_of(peer * fr_dev, fr_dev), fr_dev)],
                dst_ref=recv.at[k, pl.ds(pl.multiple_of(PAD + f * fr_dev, fr_dev), fr_dev)],
                send_sem=send_sem.at[k],
                recv_sem=recv_sem.at[k],
                device_id=(peer, p),
                device_id_type=MESH,
            ).start()
            return carry

        lax.fori_loop(1, cycles, one, 0)
        recv[k, pl.ds(pl.multiple_of(PAD + f * fr_dev, fr_dev), fr_dev), :] = send[
            k, pl.ds(pl.multiple_of(f * fr_dev, fr_dev), fr_dev), :
        ]

    pick(0)
    pl.semaphore_wait(barrier, cycles)
    ship(0)
    for k in range(1, CHUNKS):
        pick(k)
        ship(k)

    number = jnp.zeros((1, BLOCK), jnp.float32)
    for r in range(slots):
        row = (cmap[pl.ds(table[r, f], 1), :] == f).astype(jnp.float32)
        number = number + row
        mask[:, pl.ds(r * BLOCK, BLOCK)] = jnp.broadcast_to(row, (8, BLOCK))
    cnt_own[...] = jnp.broadcast_to(jnp.sum(number, axis=1, keepdims=True), (8, BLOCK))
    cnt_copy = pltpu.make_async_remote_copy(
        src_ref=cnt_own,
        dst_ref=cnt_oth,
        send_sem=cnt_sem.at[0],
        recv_sem=cnt_sem.at[1],
        device_id=(f, 1 - p),
        device_id_type=MESH,
    )
    cnt_copy.start()

    zero_pad = jnp.zeros((PAD, width), jnp.bfloat16)
    for k in range(CHUNKS):
        recv[k, pl.ds(0, PAD), :] = zero_pad
        recv[k, pl.ds(PAD + total, PAD), :] = zero_pad
    pos = lax.broadcasted_iota(jnp.int32, (total, BLOCK), 0)
    frames_in = jnp.minimum(pos + HALF_WIN, total - 1) - jnp.maximum(pos - HALF_WIN, 0) + 1
    inv_len[...] = 1.0 / frames_in.astype(jnp.float32)
    away = lax.broadcasted_iota(jnp.int32, (tile, tile + 2 * PAD), 1) - PAD - lax.broadcasted_iota(
        jnp.int32, (tile, tile + 2 * PAD), 0
    )
    band[...] = (jnp.abs(away) <= HALF_WIN).astype(jnp.float32).astype(jnp.bfloat16)
    ones_rows = jnp.ones((PAD, width), jnp.bfloat16)
    ones_cols = jnp.ones((width, BLOCK), jnp.bfloat16)
    first_row = pl.multiple_of(p * rows, rows)

    def normalise(k):
        valid = mask[0:1, pl.ds(k * width, width)] > 0.0

        for j in range(total // tile):
            start = j * tile
            summed = jnp.dot(
                band[...], recv[k, pl.ds(start, tile + 2 * PAD), :], preferred_element_type=jnp.float32
            )
            scale = inv_len[pl.ds(start, tile), :]
            mean = summed * jnp.concatenate([scale] * per, axis=1)
            value = recv[k, pl.ds(start + PAD, tile), :].astype(jnp.float32)
            normed = jnp.where(valid, value / mean, 0.0)
            own[k, pl.ds(start, tile), :] = normed.astype(jnp.bfloat16)
            pltpu.make_async_remote_copy(
                src_ref=own.at[k, pl.ds(start, tile)],
                dst_ref=oth.at[k, pl.ds(start, tile)],
                send_sem=swap_send.at[k],
                recv_sem=swap_recv.at[k],
                device_id=(f, 1 - p),
                device_id_type=MESH,
            ).start()

    def products(ref, k, n):
        left = jnp.concatenate([ref[k, pl.ds(first_row, rows), :], ones_rows], axis=0)
        return lax.dot_general(
            left,
            ref[k, pl.ds(n * tile, tile), :],
            (((1,), (1,)), ((), ())),
            preferred_element_type=jnp.float32,
        )

    def row_sums(ref, k):
        return jnp.dot(
            ref[k, pl.ds(first_row, rows), :], ones_cols, preferred_element_type=jnp.float32
        )

    def gram(ref, k, first):
        rowacc[...] = row_sums(ref, k) if first else rowacc[...] + row_sums(ref, k)
        for n in range(total // tile):
            columns = pl.ds(n * tile, tile)
            term = products(ref, k, n)
            acc[:, columns] = term if first else acc[:, columns] + term

    def swapped(k):
        pltpu.make_async_copy(own.at[k], oth.at[k], swap_recv.at[k]).wait()

    for k in range(CHUNKS):
        arrived = recv.at[k, pl.ds(0, total - fr_dev)]
        pltpu.make_async_copy(arrived, arrived, recv_sem.at[k]).wait()
        normalise(k)
        if k > 0:
            swapped(k - 1)
            gram(oth, k - 1, False)
        gram(own, k, k == 0)

    last = CHUNKS - 1
    cnt_copy.wait()
    members = cnt_own[0:1, 0:1] + cnt_oth[0:1, 0:1]
    swapped(last)
    row_total = rowacc[...] + row_sums(oth, last)
    row_total = jnp.concatenate([row_total] * (tile // BLOCK), axis=1) if tile > BLOCK else row_total[:, :tile]
    for n in range(total // tile):
        sums = acc[:, pl.ds(n * tile, tile)] + products(oth, last, n)
        col_total = sums[rows : rows + 1, :]
        result = members * sums[:rows] / (row_total * col_total) - 1.0
        out_ref[:, pl.ds(n * tile, tile)] = result.astype(jnp.bfloat16)

    for k in range(CHUNKS):
        sent = send.at[k, pl.ds(0, total - fr_dev)]
        pltpu.make_async_copy(sent, sent, send_sem.at[k]).wait()
        pltpu.make_async_copy(own.at[k], oth.at[k], swap_send.at[k]).wait()


def body(frames, cycle_map):
    fr_dev, p_sec = frames.shape
    cycles = lax.axis_size("frame")
    total = fr_dev * cycles
    blocks = p_sec // BLOCK
    rows = total // lax.axis_size("pix")
    cap = p_sec // cycles
    slots = cap // BLOCK
    width = cap // CHUNKS
    tile = min(256, total)
    dma = pltpu.SemaphoreType.DMA
    out = pl.pallas_call(
        functools.partial(kernel, cycles),
        out_shape=jax.ShapeDtypeStruct((rows, total), jnp.bfloat16),
        in_specs=[pl.BlockSpec(memory_space=pltpu.HBM)] * 2,
        out_specs=pl.BlockSpec(memory_space=pltpu.VMEM),
        scratch_shapes=[
            pltpu.VMEM((fr_dev, p_sec + BLOCK), jnp.bfloat16),
            pltpu.VMEM((blocks + 8, BLOCK), jnp.int32),
            pltpu.VMEM((slots, BLOCK), jnp.int32),
            pltpu.SMEM((slots, BLOCK), jnp.int32),
            pltpu.VMEM((CHUNKS, total, width), jnp.bfloat16),
            pltpu.VMEM((CHUNKS, total + 2 * PAD, width), jnp.bfloat16),
            pltpu.VMEM((CHUNKS, total, width), jnp.bfloat16),
            pltpu.VMEM((CHUNKS, total, width), jnp.bfloat16),
            pltpu.VMEM((rows + PAD, total), jnp.float32),
            pltpu.VMEM((rows, BLOCK), jnp.float32),
            pltpu.VMEM((total, BLOCK), jnp.float32),
            pltpu.VMEM((tile, tile + 2 * PAD), jnp.bfloat16),
            pltpu.VMEM((8, cap), jnp.float32),
            pltpu.VMEM((8, BLOCK), jnp.float32),
            pltpu.VMEM((8, BLOCK), jnp.float32),
            dma((3,)),
            dma((CHUNKS,)),
            dma((CHUNKS,)),
            dma((CHUNKS,)),
            dma((CHUNKS,)),
            dma((2,)),
        ],
        compiler_params=pltpu.CompilerParams(
            collective_id=0, has_side_effects=True, vmem_limit_bytes=60 << 20
        ),
    )(frames, cycle_map.reshape(blocks, BLOCK))
    return out[None]


def solution(mesh):
    return jax.shard_map(
        body,
        mesh=mesh,
        in_specs=(P("frame", "pix"), P("pix")),
        out_specs=P("frame", "pix", None),
        check_vma=False,
    )
```

time: 108 us -> 42.8 us (0.40)
  blocking collectives: 47.9 us -> 0 us
  Pallas kernels: 0 us -> 40.3 us
  between operations: 13.5 us -> 0.01 us
  waiting for transfers between devices: 11 us -> 0 us
  other arithmetic: 10 us -> 0 us
  local copies, waits for them, and re-layouts: 12.2 us -> 2.26 us
  matrix products: 7.29 us -> 0 us
  starting transfers between devices: 5.25 us -> 0 us
    all_to_all x1 -> x0, blocking collectives: 41.8 us -> none  [body(): lax.all_to_all(picked, 'frame', split_axis=1, concat_axis=0, tiled=True)]
    pallas_call x0 -> x1, Pallas kernels: none -> 40.3 us  [body(): pl.pallas_call(functools.partial(kernel, cycles), out_shape=jax.ShapeDtyp...]
    dot_general x3 -> x0, matrix products: 7.29 us -> none  [the longest x1 4.3 us: body(): lax.dot_general(received, received, (((1,), (1,)), ((), ())), preferred_e...]
    psum x1 -> x0, blocking collectives: 6.08 us -> none  [body(): lax.psum((jnp.sum(received, axis=1, dtype=jnp.float32), own_count), 'pix')]
    reduce_scatter x1 -> x0, waiting for transfers between devices: 6 us -> none  [body(): lax.psum_scatter(lax.dot_general(received, received, (((1,), (1,)), ((),...]
    ppermute x2 -> x0, starting transfers between devices: 5.25 us -> none  [the longest x1 3.96 us: with_halo(): before = lax.ppermute(last, axis, up)]
    all_to_all x2 -> x0, local copies, waits for them, and re-layouts: 5.07 us -> none  [body(): lax.all_to_all(picked, 'frame', split_axis=1, concat_axis=0, tiled=True)]
    ppermute x2 -> x0, waiting for transfers between devices: 5.02 us -> none  [the longest x1 3.81 us: with_halo(): after = lax.ppermute(initial, axis, down)]
  transfers between devices with their start and end apart: 3 -> 0, of which waited for: 3 -> 0; matrix products, arithmetic and copies ran while one was open for 3% -> 0% of each run, Pallas kernels for 0% -> 0%
where the time goes in v1:
time: 42.8 us; the launch traced here: 42.6 us
  Pallas kernels  40.3 us (94%)
  local copies, waits for them, and re-layouts  2.26 us (5%)
    pallas_call x1, Pallas kernels, body(): pl.pallas_call(functools.partial(kernel, cycles), out_shape=jax.ShapeDtyp...  40.3 us
    unnamed x1, local copies, waits for them, and re-layouts  2.26 us

profile of v1, /device:TPU:1, one launch (start us, length us, event | category | flops | bytes accessed | tf_op | source)
XLA Modules:
  0.0 42.6 jit_solution(2048461100011049059)
XLA Ops:
  0.0 40.3 %shard_map.28 = bf16[512,1024]{1,0:T(8,128)(2,1)} custom-call(bf16[16,65536]{1,0:T(8,128)(2,1)} %frames_hbm.1, s32[512,128]{1,0:T(8,128)} %bitcast.3), custom_call_target="tpu_custom_call" | custom-call | tf_op jit(solution)/shard_map/pallas_call | solution.py:251
  40.3 2.3 %copy.4 = bf16[1,512,1024]{2,1,0:T(8,128)(2,1)} copy(bf16[1,512,1024]{2,1,0:T(8,128)(2,1)} %bitcast.2) | data formatting | bytes 2097152

commit v2 on v1

--- a/solution.py
+++ b/solution.py
@@ -10,9 +10,14 @@
 BLOCK = 128
 HALF_WIN = 2
 PAD = 16
-CHUNKS = 4
+SPLIT = (3, 3, 2)
 STRIDE = 27
 MESH = pl.DeviceIdType.MESH
+
+
+def chunks_of(slots):
+    sizes = [size * slots // sum(SPLIT) for size in SPLIT]
+    return [(sum(sizes[:k]), size) for k, size in enumerate(sizes)]
 
 
 def kernel(
@@ -24,23 +29,7 @@
     cmap,
     table_v,
     table,
-    send,
-    recv,
-    own,
-    oth,
-    acc,
-    rowacc,
-    inv_len,
-    band,
-    mask,
-    cnt_own,
-    cnt_oth,
-    load_sem,
-    send_sem,
-    recv_sem,
-    swap_send,
-    swap_recv,
-    cnt_sem,
+    *refs,
 ):
     f = lax.axis_index("frame")
     p = lax.axis_index("pix")
@@ -50,9 +39,25 @@
     total = fr_dev * cycles
     rows = total // 2
     slots = p_sec // cycles // BLOCK
-    per = slots // CHUNKS
-    width = per * BLOCK
+    chunks = chunks_of(slots)
+    count = len(chunks)
     tile = min(256, total)
+    send, recv, own, oth = (refs[i * count : (i + 1) * count] for i in range(4))
+    (
+        acc,
+        rowacc,
+        inv_len,
+        band,
+        mask,
+        cnt_own,
+        cnt_oth,
+        load_sem,
+        send_sem,
+        recv_sem,
+        swap_send,
+        swap_recv,
+        cnt_sem,
+    ) = refs[4 * count :]
 
     map_copy = pltpu.make_async_copy(map_hbm, cmap.at[pl.ds(0, blocks)], load_sem.at[0])
     map_copy.start()
@@ -99,9 +104,9 @@
 
     def pick(k):
         def one(q, carry):
-            for j in range(per):
-                b = table[k * per + j, q]
-                send[k, pl.ds(pl.multiple_of(q * fr_dev, fr_dev), fr_dev), pl.ds(j * BLOCK, BLOCK)] = fr[
+            for j in range(chunks[k][1]):
+                b = table[chunks[k][0] + j, q]
+                send[k][pl.ds(pl.multiple_of(q * fr_dev, fr_dev), fr_dev), pl.ds(j * BLOCK, BLOCK)] = fr[
                     :, pl.ds(b * BLOCK, BLOCK)
                 ]
             return carry
@@ -112,8 +117,8 @@
         def one(i, carry):
             peer = lax.rem(f + STRIDE * i, cycles)
             pltpu.make_async_remote_copy(
-                src_ref=send.at[k, pl.ds(pl.multiple_of(peer * fr_dev, fr_dev), fr_dev)],
-                dst_ref=recv.at[k, pl.ds(pl.multiple_of(PAD + f * fr_dev, fr_dev), fr_dev)],
+                src_ref=send[k].at[pl.ds(pl.multiple_of(peer * fr_dev, fr_dev), fr_dev)],
+                dst_ref=recv[k].at[pl.ds(pl.multiple_of(PAD + f * fr_dev, fr_dev), fr_dev)],
                 send_sem=send_sem.at[k],
                 recv_sem=recv_sem.at[k],
                 device_id=(peer, p),
@@ -122,14 +127,14 @@
             return carry
 
         lax.fori_loop(1, cycles, one, 0)
-        recv[k, pl.ds(pl.multiple_of(PAD + f * fr_dev, fr_dev), fr_dev), :] = send[
-            k, pl.ds(pl.multiple_of(f * fr_dev, fr_dev), fr_dev), :
+        recv[k][pl.ds(pl.multiple_of(PAD + f * fr_dev, fr_dev), fr_dev), :] = send[k][
+            pl.ds(pl.multiple_of(f * fr_dev, fr_dev), fr_dev), :
         ]
 
     pick(0)
     pl.semaphore_wait(barrier, cycles)
     ship(0)
-    for k in range(1, CHUNKS):
+    for k in range(1, count):
         pick(k)
         ship(k)
 
@@ -149,10 +154,10 @@
     )
     cnt_copy.start()
 
-    zero_pad = jnp.zeros((PAD, width), jnp.bfloat16)
-    for k in range(CHUNKS):
-        recv[k, pl.ds(0, PAD), :] = zero_pad
-        recv[k, pl.ds(PAD + total, PAD), :] = zero_pad
+    for k in range(count):
+        zero_pad = jnp.zeros((PAD, chunks[k][1] * BLOCK), jnp.bfloat16)
+        recv[k][pl.ds(0, PAD), :] = zero_pad
+        recv[k][pl.ds(PAD + total, PAD), :] = zero_pad
     pos = lax.broadcasted_iota(jnp.int32, (total, BLOCK), 0)
     frames_in = jnp.minimum(pos + HALF_WIN, total - 1) - jnp.maximum(pos - HALF_WIN, 0) + 1
     inv_len[...] = 1.0 / frames_in.astype(jnp.float32)
@@ -160,26 +165,24 @@
         jnp.int32, (tile, tile + 2 * PAD), 0
     )
     band[...] = (jnp.abs(away) <= HALF_WIN).astype(jnp.float32).astype(jnp.bfloat16)
-    ones_rows = jnp.ones((PAD, width), jnp.bfloat16)
-    ones_cols = jnp.ones((width, BLOCK), jnp.bfloat16)
     first_row = pl.multiple_of(p * rows, rows)
 
     def normalise(k):
-        valid = mask[0:1, pl.ds(k * width, width)] > 0.0
+        valid = mask[0:1, pl.ds(chunks[k][0] * BLOCK, chunks[k][1] * BLOCK)] > 0.0
 
         for j in range(total // tile):
             start = j * tile
             summed = jnp.dot(
-                band[...], recv[k, pl.ds(start, tile + 2 * PAD), :], preferred_element_type=jnp.float32
+                band[...], recv[k][pl.ds(start, tile + 2 * PAD), :], preferred_element_type=jnp.float32
             )
             scale = inv_len[pl.ds(start, tile), :]
-            mean = summed * jnp.concatenate([scale] * per, axis=1)
-            value = recv[k, pl.ds(start + PAD, tile), :].astype(jnp.float32)
+            mean = summed * jnp.concatenate([scale] * chunks[k][1], axis=1)
+            value = recv[k][pl.ds(start + PAD, tile), :].astype(jnp.float32)
             normed = jnp.where(valid, value / mean, 0.0)
-            own[k, pl.ds(start, tile), :] = normed.astype(jnp.bfloat16)
+            own[k][pl.ds(start, tile), :] = normed.astype(jnp.bfloat16)
             pltpu.make_async_remote_copy(
-                src_ref=own.at[k, pl.ds(start, tile)],
-                dst_ref=oth.at[k, pl.ds(start, tile)],
+                src_ref=own[k].at[pl.ds(start, tile)],
+                dst_ref=oth[k].at[pl.ds(start, tile)],
                 send_sem=swap_send.at[k],
                 recv_sem=swap_recv.at[k],
                 device_id=(f, 1 - p),
@@ -187,17 +190,19 @@
             ).start()
 
     def products(ref, k, n):
-        left = jnp.concatenate([ref[k, pl.ds(first_row, rows), :], ones_rows], axis=0)
+        ones_rows = jnp.ones((PAD, ref[k].shape[1]), jnp.bfloat16)
+        left = jnp.concatenate([ref[k][pl.ds(first_row, rows), :], ones_rows], axis=0)
         return lax.dot_general(
             left,
-            ref[k, pl.ds(n * tile, tile), :],
+            ref[k][pl.ds(n * tile, tile), :],
             (((1,), (1,)), ((), ())),
             preferred_element_type=jnp.float32,
         )
 
     def row_sums(ref, k):
+        ones_cols = jnp.ones((ref[k].shape[1], BLOCK), jnp.bfloat16)
         return jnp.dot(
-            ref[k, pl.ds(first_row, rows), :], ones_cols, preferred_element_type=jnp.float32
+            ref[k][pl.ds(first_row, rows), :], ones_cols, preferred_element_type=jnp.float32
         )
 
     def gram(ref, k, first):
@@ -208,10 +213,10 @@
             acc[:, columns] = term if first else acc[:, columns] + term
 
     def swapped(k):
-        pltpu.make_async_copy(own.at[k], oth.at[k], swap_recv.at[k]).wait()
-
-    for k in range(CHUNKS):
-        arrived = recv.at[k, pl.ds(0, total - fr_dev)]
+        pltpu.make_async_copy(own[k], oth[k], swap_recv.at[k]).wait()
+
+    for k in range(count):
+        arrived = recv[k].at[pl.ds(0, total - fr_dev)]
         pltpu.make_async_copy(arrived, arrived, recv_sem.at[k]).wait()
         normalise(k)
         if k > 0:
@@ -219,7 +224,7 @@
             gram(oth, k - 1, False)
         gram(own, k, k == 0)
 
-    last = CHUNKS - 1
+    last = count - 1
     cnt_copy.wait()
     members = cnt_own[0:1, 0:1] + cnt_oth[0:1, 0:1]
     swapped(last)
@@ -231,10 +236,10 @@
         result = members * sums[:rows] / (row_total * col_total) - 1.0
         out_ref[:, pl.ds(n * tile, tile)] = result.astype(jnp.bfloat16)
 
-    for k in range(CHUNKS):
-        sent = send.at[k, pl.ds(0, total - fr_dev)]
+    for k in range(count):
+        sent = send[k].at[pl.ds(0, total - fr_dev)]
         pltpu.make_async_copy(sent, sent, send_sem.at[k]).wait()
-        pltpu.make_async_copy(own.at[k], oth.at[k], swap_send.at[k]).wait()
+        pltpu.make_async_copy(own[k], oth[k], swap_send.at[k]).wait()
 
 
 def body(frames, cycle_map):
@@ -245,12 +250,13 @@
     rows = total // lax.axis_size("pix")
     cap = p_sec // cycles
     slots = cap // BLOCK
-    width = cap // CHUNKS
+    chunks = chunks_of(slots)
+    widths = [size * BLOCK for first, size in chunks]
     tile = min(256, total)
     dma = pltpu.SemaphoreType.DMA
     out = pl.pallas_call(
         functools.partial(kernel, cycles),
-        out_shape=jax.ShapeDtypeStruct((rows, total), jnp.bfloat16),
+        out_shape=pltpu.VMEM((rows, total), jnp.bfloat16),
         in_specs=[pl.BlockSpec(memory_space=pltpu.HBM)] * 2,
         out_specs=pl.BlockSpec(memory_space=pltpu.VMEM),
         scratch_shapes=[
@@ -258,10 +264,10 @@
             pltpu.VMEM((blocks + 8, BLOCK), jnp.int32),
             pltpu.VMEM((slots, BLOCK), jnp.int32),
             pltpu.SMEM((slots, BLOCK), jnp.int32),
-            pltpu.VMEM((CHUNKS, total, width), jnp.bfloat16),
-            pltpu.VMEM((CHUNKS, total + 2 * PAD, width), jnp.bfloat16),
-            pltpu.VMEM((CHUNKS, total, width), jnp.bfloat16),
-            pltpu.VMEM((CHUNKS, total, width), jnp.bfloat16),
+            *[pltpu.VMEM((total, width), jnp.bfloat16) for width in widths],
+            *[pltpu.VMEM((total + 2 * PAD, width), jnp.bfloat16) for width in widths],
+            *[pltpu.VMEM((total, width), jnp.bfloat16) for width in widths],
+            *[pltpu.VMEM((total, width), jnp.bfloat16) for width in widths],
             pltpu.VMEM((rows + PAD, total), jnp.float32),
             pltpu.VMEM((rows, BLOCK), jnp.float32),
             pltpu.VMEM((total, BLOCK), jnp.float32),
@@ -270,10 +276,10 @@
             pltpu.VMEM((8, BLOCK), jnp.float32),
             pltpu.VMEM((8, BLOCK), jnp.float32),
             dma((3,)),
-            dma((CHUNKS,)),
-            dma((CHUNKS,)),
-            dma((CHUNKS,)),
-            dma((CHUNKS,)),
+            dma((len(chunks),)),
+            dma((len(chunks),)),
+            dma((len(chunks),)),
+            dma((len(chunks),)),
             dma((2,)),
         ],
         compiler_params=pltpu.CompilerParams(

time: 42.8 us -> 40.3 us (0.942)
  local copies, waits for them, and re-layouts: 2.26 us -> 0.97 us
  Pallas kernels: 40.3 us -> 39.2 us
    unnamed x1, local copies, waits for them, and re-layouts: 2.26 us -> 0.97 us
    pallas_call x1, Pallas kernels: 40.3 us -> 39.2 us  [body(): pl.pallas_call(functools.partial(kernel, cycles), out_shape=pltpu.VMEM((r...]
where the time goes in v2:
time: 40.3 us; the launch traced here: 40.2 us
  Pallas kernels  39.2 us (97%)
  local copies, waits for them, and re-layouts  0.97 us (2%)
    pallas_call x1, Pallas kernels, body(): pl.pallas_call(functools.partial(kernel, cycles), out_shape=pltpu.VMEM((r...  39.2 us
    unnamed x1, local copies, waits for them, and re-layouts  0.97 us

profile of v2, /device:TPU:1, one launch (start us, length us, event | category | flops | bytes accessed | tf_op | source)
XLA Modules:
  0.0 40.2 jit_solution(8776572780208868293)
XLA Ops:
  0.0 39.2 %shard_map.28 = bf16[512,1024]{1,0:T(8,128)(2,1)S(1)} custom-call(bf16[16,65536]{1,0:T(8,128)(2,1)} %frames_hbm.1, s32[512,128]{1,0:T(8,128)} %bitcast.3), custom_call_target="tpu_custom_call" | custom-call | tf_op jit(solution)/shard_map/pallas_call | solution.py:257
  39.2 1.0 %copy.4 = bf16[1,512,1024]{2,1,0:T(8,128)(2,1)} copy(bf16[1,512,1024]{2,1,0:T(8,128)(2,1)S(1)} %bitcast.2) | data formatting | bytes 2097152

commit v3 on v2

--- a/solution.py
+++ b/solution.py
@@ -10,7 +10,7 @@
 BLOCK = 128
 HALF_WIN = 2
 PAD = 16
-SPLIT = (3, 3, 2)
+SPLIT = (2, 2, 2, 2)
 STRIDE = 27
 MESH = pl.DeviceIdType.MESH
 
@@ -71,7 +71,8 @@
         pl.semaphore_signal(barrier, inc=1, device_id=(peer, p), device_id_type=MESH)
         return carry
 
-    lax.fori_loop(1, cycles, greet, 0)
+    steps = 7 if cycles % 7 == 1 else 1
+    lax.fori_loop(1, cycles, greet, 0, unroll=steps)
     pl.semaphore_signal(barrier, inc=1, device_id=(f, 1 - p), device_id_type=MESH)
 
     fr[:, pl.ds(p_sec, BLOCK)] = jnp.zeros((fr_dev, BLOCK), jnp.bfloat16)
@@ -126,7 +127,7 @@
             ).start()
             return carry
 
-        lax.fori_loop(1, cycles, one, 0)
+        lax.fori_loop(1, cycles, one, 0, unroll=steps)
         recv[k][pl.ds(pl.multiple_of(PAD + f * fr_dev, fr_dev), fr_dev), :] = send[k][
             pl.ds(pl.multiple_of(f * fr_dev, fr_dev), fr_dev), :
         ]
@@ -189,27 +190,29 @@
                 device_id_type=MESH,
             ).start()
 
-    def products(ref, k, n):
-        ones_rows = jnp.ones((PAD, ref[k].shape[1]), jnp.bfloat16)
-        left = jnp.concatenate([ref[k][pl.ds(first_row, rows), :], ones_rows], axis=0)
+    def side_by_side(parts, start, length):
+        return jnp.concatenate([ref[pl.ds(start, length), :] for ref in parts], axis=1)
+
+    def products(parts, n):
+        left = side_by_side(parts, first_row, rows)
+        ones_rows = jnp.ones((PAD, left.shape[1]), jnp.bfloat16)
         return lax.dot_general(
-            left,
-            ref[k][pl.ds(n * tile, tile), :],
+            jnp.concatenate([left, ones_rows], axis=0),
+            side_by_side(parts, n * tile, tile),
             (((1,), (1,)), ((), ())),
             preferred_element_type=jnp.float32,
         )
 
-    def row_sums(ref, k):
-        ones_cols = jnp.ones((ref[k].shape[1], BLOCK), jnp.bfloat16)
-        return jnp.dot(
-            ref[k][pl.ds(first_row, rows), :], ones_cols, preferred_element_type=jnp.float32
-        )
-
-    def gram(ref, k, first):
-        rowacc[...] = row_sums(ref, k) if first else rowacc[...] + row_sums(ref, k)
+    def row_sums(parts):
+        left = side_by_side(parts, first_row, rows)
+        ones_cols = jnp.ones((left.shape[1], BLOCK), jnp.bfloat16)
+        return jnp.dot(left, ones_cols, preferred_element_type=jnp.float32)
+
+    def gram(parts, first):
+        rowacc[...] = row_sums(parts) if first else rowacc[...] + row_sums(parts)
         for n in range(total // tile):
             columns = pl.ds(n * tile, tile)
-            term = products(ref, k, n)
+            term = products(parts, n)
             acc[:, columns] = term if first else acc[:, columns] + term
 
     def swapped(k):
@@ -221,20 +224,22 @@
         normalise(k)
         if k > 0:
             swapped(k - 1)
-            gram(oth, k - 1, False)
-        gram(own, k, k == 0)
+        gram([own[k]] if k == 0 else [oth[k - 1], own[k]], k == 0)
 
     last = count - 1
     cnt_copy.wait()
     members = cnt_own[0:1, 0:1] + cnt_oth[0:1, 0:1]
     swapped(last)
-    row_total = rowacc[...] + row_sums(oth, last)
-    row_total = jnp.concatenate([row_total] * (tile // BLOCK), axis=1) if tile > BLOCK else row_total[:, :tile]
+    row_total = rowacc[...] + row_sums([oth[last]])
+    if tile > BLOCK:
+        row_total = jnp.concatenate([row_total] * (tile // BLOCK), axis=1)
+    else:
+        row_total = row_total[:, :tile]
     for n in range(total // tile):
-        sums = acc[:, pl.ds(n * tile, tile)] + products(oth, last, n)
-        col_total = sums[rows : rows + 1, :]
-        result = members * sums[:rows] / (row_total * col_total) - 1.0
-        out_ref[:, pl.ds(n * tile, tile)] = result.astype(jnp.bfloat16)
+        columns = pl.ds(n * tile, tile)
+        sums = acc[:, columns] + products([oth[last]], n)
+        result = members * sums[:rows] / (row_total * sums[rows : rows + 1, :]) - 1.0
+        out_ref[:, columns] = result.astype(jnp.bfloat16)
 
     for k in range(count):
         sent = send[k].at[pl.ds(0, total - fr_dev)]

time: 40.3 us -> 40.3 us (level)
  no operation moved by 1% of the time
where the time goes in v3:
time: 40.3 us; the launch traced here: 40.1 us
  Pallas kernels  39.2 us (97%)
  local copies, waits for them, and re-layouts  0.97 us (2%)
    pallas_call x1, Pallas kernels, body(): pl.pallas_call(functools.partial(kernel, cycles), out_shape=pltpu.VMEM((r...  39.2 us
    unnamed x1, local copies, waits for them, and re-layouts  0.97 us

profile of v3, /device:TPU:1, one launch (start us, length us, event | category | flops | bytes accessed | tf_op | source)
XLA Modules:
  0.0 40.1 jit_solution(10094731767578963217)
XLA Ops:
  0.0 39.2 %shard_map.28 = bf16[512,1024]{1,0:T(8,128)(2,1)S(1)} custom-call(bf16[16,65536]{1,0:T(8,128)(2,1)} %frames_hbm.1, s32[512,128]{1,0:T(8,128)} %bitcast.3), custom_call_target="tpu_custom_call" | custom-call | tf_op jit(solution)/shard_map/pallas_call | solution.py:262
  39.2 1.0 %copy.4 = bf16[1,512,1024]{2,1,0:T(8,128)(2,1)} copy(bf16[1,512,1024]{2,1,0:T(8,128)(2,1)S(1)} %bitcast.2) | data formatting | bytes 2097152

commit v4 on v3

--- a/solution.py
+++ b/solution.py
@@ -11,7 +11,7 @@
 HALF_WIN = 2
 PAD = 16
 SPLIT = (2, 2, 2, 2)
-STRIDE = 27
+STRIDE = 11
 MESH = pl.DeviceIdType.MESH
 
 

time: 40.3 us -> 40.1 us (level)
  no operation moved by 1% of the time
where the time goes in v4:
time: 40.1 us; the launch traced here: 40 us
  Pallas kernels  39 us (97%)
  local copies, waits for them, and re-layouts  0.97 us (2%)
    pallas_call x1, Pallas kernels, body(): pl.pallas_call(functools.partial(kernel, cycles), out_shape=pltpu.VMEM((r...  39 us
    unnamed x1, local copies, waits for them, and re-layouts  0.97 us

profile of v4, /device:TPU:1, one launch (start us, length us, event | category | flops | bytes accessed | tf_op | source)
XLA Modules:
  0.0 40.0 jit_solution(10944323133375977611)
XLA Ops:
  0.0 39.0 %shard_map.28 = bf16[512,1024]{1,0:T(8,128)(2,1)S(1)} custom-call(bf16[16,65536]{1,0:T(8,128)(2,1)} %frames_hbm.1, s32[512,128]{1,0:T(8,128)} %bitcast.3), custom_call_target="tpu_custom_call" | custom-call | tf_op jit(solution)/shard_map/pallas_call | solution.py:262
  39.0 1.0 %copy.4 = bf16[1,512,1024]{2,1,0:T(8,128)(2,1)} copy(bf16[1,512,1024]{2,1,0:T(8,128)(2,1)S(1)} %bitcast.2) | data formatting | bytes 2097152

commit v5 on v4

--- a/solution.py
+++ b/solution.py
@@ -10,7 +10,7 @@
 BLOCK = 128
 HALF_WIN = 2
 PAD = 16
-SPLIT = (2, 2, 2, 2)
+SPLIT = (3, 3, 2)
 STRIDE = 11
 MESH = pl.DeviceIdType.MESH
 

time: 40.1 us -> 40 us (level)
  no operation moved by 1% of the time
where the time goes in v5:
time: 40 us; the launch traced here: 39.9 us
  Pallas kernels  38.9 us (97%)
  local copies, waits for them, and re-layouts  0.97 us (2%)
    pallas_call x1, Pallas kernels, body(): pl.pallas_call(functools.partial(kernel, cycles), out_shape=pltpu.VMEM((r...  38.9 us
    unnamed x1, local copies, waits for them, and re-layouts  0.97 us

profile of v5, /device:TPU:1, one launch (start us, length us, event | category | flops | bytes accessed | tf_op | source)
XLA Modules:
  0.0 39.9 jit_solution(13015788588341036528)
XLA Ops:
  0.0 38.9 %shard_map.28 = bf16[512,1024]{1,0:T(8,128)(2,1)S(1)} custom-call(bf16[16,65536]{1,0:T(8,128)(2,1)} %frames_hbm.1, s32[512,128]{1,0:T(8,128)} %bitcast.3), custom_call_target="tpu_custom_call" | custom-call | tf_op jit(solution)/shard_map/pallas_call | solution.py:262
  38.9 1.0 %copy.4 = bf16[1,512,1024]{2,1,0:T(8,128)(2,1)} copy(bf16[1,512,1024]{2,1,0:T(8,128)(2,1)S(1)} %bitcast.2) | data formatting | bytes 2097152
